TPU v7x, 256 devices: a whole 4x4x8 slice. The times are simulated.
256 devices in a mesh: dp: 8 (over z_lo, x), ctx: 32 (over z_hi, y, core).
Axes of the slice: x: 4, y: 4, z: 8 (z_hi: 4, z_lo: 2; z = z_hi * 2 + z_lo), core: 2. Of those that a mesh axis runs over, the one named last changes fastest.
Arguments:
- tokens: bfloat16 [8, 4096, 4096], P('dp', 'ctx'), may hold values from -6 to 6
- proj_weight: bfloat16 [4096, 512], P('dp'), may hold values from -0.09375 to 0.09375
- values: bfloat16 [8, 4096, 2048], P('dp', 'ctx'), may hold values from -60 to 60
- grad_out: bfloat16 [8, 4096, 2048], P('dp', 'ctx'), may hold values from -6 to 6
Outputs:
- attended: bfloat16 [8, 4096, 2048], P('dp', 'ctx')
- grad_tokens: bfloat16 [8, 4096, 4096], P('dp', 'ctx')
- grad_values: bfloat16 [8, 4096, 2048], P('dp', 'ctx')
- grad_proj: float32 [4096, 512], P(('dp', 'ctx'))
All inputs are finite; a program needn't handle non-finite values.
Results may differ from a plain program's by a relative error of at most 0.0049.
Values may be sent and summed in bfloat16 or wider, within the bound.
A program may use at most 192 MiB of HBM per device.

v0:
```python
import jax
import jax.numpy as jnp
from jax import lax
from jax.sharding import PartitionSpec as P

H = 16
F = 16
DH = 128
HIGHEST = lax.Precision.HIGHEST
QUAD_SCALE = 0.17677669529663687
EPSILON = 1e-05


def features(inputs):
    count_heads, count_rows, count_feat = inputs.shape
    linear = jnp.swapaxes(inputs, 1, 2) * 0.5
    square = (inputs[:, :, :, None] * inputs[:, :, None, :]).reshape(
        count_heads, count_rows, count_feat * count_feat
    )
    square = jnp.swapaxes(square, 1, 2) * QUAD_SCALE
    constant_row = jnp.ones((count_heads, 1, count_rows), inputs.dtype)
    return jnp.concatenate([constant_row, linear, square], axis=1)


def block_kernel(query_part, key_part):
    count_rows = query_part.shape[1]
    causal = lax.broadcasted_iota(jnp.int32, (count_rows, count_rows), 0) >= lax.broadcasted_iota(
        jnp.int32, (count_rows, count_rows), 1
    )
    scores = jnp.einsum("htf,hsf->hts", query_part, key_part, precision=HIGHEST) * 0.25
    kernel = jnp.where(causal, 1.0 + scores + 0.5 * scores * scores, 0.0)
    return (causal, scores, kernel)


def normalize(numerator):
    inv_rms = lax.rsqrt(jnp.mean(numerator * numerator, axis=-1, keepdims=True) + EPSILON)
    return (inv_rms, numerator * inv_rms)


def grad_normalize(inv_rms, normed, upstream):
    return inv_rms * (upstream - normed * jnp.mean(normed * upstream, axis=-1, keepdims=True))


def local_backward(
    query_part,
    key_part,
    value_part,
    grad_num,
    causal,
    scores,
    kernel,
    pull_query,
    pull_key,
    feat_key,
    prefix,
    suffix,
):
    mixing = jnp.where(
        causal, jnp.einsum("htd,hsd->hts", grad_num, value_part, precision=HIGHEST), 0.0
    )
    slope = mixing * (1.0 + scores)
    grad_query = jnp.einsum("hts,hsf->htf", slope, key_part, precision=HIGHEST) * 0.25
    grad_key = jnp.einsum("hts,htf->hsf", slope, query_part, precision=HIGHEST) * 0.25
    grad_query = (
        grad_query + pull_query(jnp.einsum("hed,htd->het", prefix, grad_num, precision=HIGHEST))[0]
    )
    grad_key = (
        grad_key + pull_key(jnp.einsum("hed,htd->het", suffix, value_part, precision=HIGHEST))[0]
    )
    grad_value = jnp.einsum("hts,htd->hsd", kernel, grad_num, precision=HIGHEST)
    grad_value = grad_value + jnp.einsum("het,hed->htd", feat_key, suffix, precision=HIGHEST)
    return (grad_query, grad_key, grad_value)


def exclusive(blocks, later):
    count = blocks.shape[0]
    row = lax.broadcasted_iota(jnp.int32, (count, count), 0)
    col = lax.broadcasted_iota(jnp.int32, (count, count), 1)
    chosen = col > row if later else col < row
    return jnp.dot(chosen.astype(jnp.float32), blocks, precision=HIGHEST)


def split_heads(matrix, size):
    return jnp.swapaxes(matrix.reshape(matrix.shape[0], -1, size), 0, 1)


def merge_heads(blocked):
    return jnp.swapaxes(blocked, 0, 1).reshape(blocked.shape[1], -1)


def local(tokens, proj_weight, values, grad_out):
    token_rows = tokens[0]
    query_cols = H * F
    tokens_cols = lax.all_to_all(token_rows, "dp", split_axis=1, concat_axis=0, tiled=True)
    projected = jnp.dot(
        token_rows,
        lax.all_gather(proj_weight, "dp", axis=0, tiled=True),
        preferred_element_type=jnp.float32,
    )
    query_part = split_heads(projected[:, :query_cols], F)
    key_part = split_heads(projected[:, query_cols:], F)
    value_part = split_heads(values[0].astype(jnp.float32), DH)
    upstream = split_heads(grad_out[0].astype(jnp.float32), DH)
    feat_query, pull_query = jax.vjp(features, query_part)
    feat_key, pull_key = jax.vjp(features, key_part)
    local_term = jnp.einsum("het,htd->hed", feat_key, value_part, precision=HIGHEST)
    columns_in = lax.all_to_all(
        local_term.reshape(1, -1), "ctx", split_axis=1, concat_axis=0, tiled=True
    )
    running = exclusive(columns_in, False)
    prefix = lax.all_to_all(running, "ctx", split_axis=0, concat_axis=1, tiled=True).reshape(
        local_term.shape
    )
    causal, scores, kernel = block_kernel(query_part, key_part)
    numerator = jnp.einsum("hts,hsd->htd", kernel, value_part, precision=HIGHEST)
    numerator = numerator + jnp.einsum("het,hed->htd", feat_query, prefix, precision=HIGHEST)
    inv_rms, normed = normalize(numerator)
    attended = merge_heads(normed).astype(jnp.bfloat16)
    grad_num = grad_normalize(inv_rms, normed, upstream)
    carried = jnp.einsum("het,htd->hed", feat_query, grad_num, precision=HIGHEST)
    later_in = lax.all_to_all(
        carried.reshape(1, -1), "ctx", split_axis=1, concat_axis=0, tiled=True
    )
    later_running = exclusive(later_in, True)
    suffix = lax.all_to_all(later_running, "ctx", split_axis=0, concat_axis=1, tiled=True).reshape(
        carried.shape
    )
    grad_query, grad_key, grad_value = local_backward(
        query_part,
        key_part,
        value_part,
        grad_num,
        causal,
        scores,
        kernel,
        pull_query,
        pull_key,
        feat_key,
        prefix,
        suffix,
    )
    grad_proj_rows = jnp.concatenate(
        [merge_heads(grad_query), merge_heads(grad_key)], axis=1
    ).astype(jnp.bfloat16)
    grad_tokens = lax.dot_general(
        grad_proj_rows,
        lax.all_gather(proj_weight, "dp", axis=0, tiled=True),
        (((1,), (1,)), ((), ())),
        preferred_element_type=jnp.float32,
    ).astype(jnp.bfloat16)
    rows_all = lax.all_gather(grad_proj_rows, "dp", axis=0, tiled=True)
    grad_proj = lax.psum_scatter(
        lax.dot_general(
            tokens_cols, rows_all, (((0,), (0,)), ((), ())), preferred_element_type=jnp.float32
        ),
        "ctx",
        scatter_dimension=0,
        tiled=True,
    )
    grad_values = merge_heads(grad_value).astype(jnp.bfloat16)
    return (attended[None], grad_tokens[None], grad_values[None], grad_proj)


def solution(mesh):
    return jax.shard_map(
        local,
        mesh=mesh,
        in_specs=(P("dp", "ctx", None), P("dp", None), P("dp", "ctx", None), P("dp", "ctx", None)),
        out_specs=(
            P("dp", "ctx", None),
            P("dp", "ctx", None),
            P("dp", "ctx", None),
            P(("dp", "ctx"), None),
        ),
        check_vma=False,
    )
```

profile of v0, /device:TPU:2, one launch (start us, length us, event | category | flops | bytes accessed | tf_op | source)
XLA Modules:
  0.0 523.0 jit_solution(1464538950625554450)
XLA Ops:
  7.9 1.1 copy.72
  9.1 56.6 %all-gather.3.cloned.1.call-done = bf16[4096,512]{1,0:T(8,128)(2,1)} async-done(((bf16[512,512]{1,0:T(8,128)(2,1)}), bf16[4096,512]{1,0:T(8,128)(2,1)}) %all-gather.3.cloned.1.call-update) | async-done | bytes 4194320 | tf_op jit(solution)/shard_map/all_gather | solution.py:97
  65.7 3.2 fusion.22
  69.4 1.4 copy-done.1
  70.8 2.1 fusion.6
  72.9 3.7 all_to_all.72
  76.6 65.7 %all_to_all.79 = f32[1,32,17472]{2,0,1:T(1,128)S(1)} all-to-all(f32[1,32,17472]{2,0,1:T(1,128)} %all_to_all.72), channel_id=1, replica_groups=mesh['dp'=8,'ctx'=32] {'ctx'}, dimensions={1} | all-to-all | bytes 4472832 | tf_op jit(solution)/shard_map/all_to_all | solution.py:107
  142.3 1.2 convolution_bitcast_fusion.1
  143.5 3.7 copy.50
  147.2 4.5 all-to-all-start.1
  151.8 1.2 copy.51
  153.8 2.7 fusion.60
  156.5 2.9 multiply_multiply_fusion.1
  159.5 46.6 %all-to-all-done.1 = f32[32,1,17472]{2,1,0:T(1,128)S(1)} async-done(((f32[32,1,17472]{2,1,0:T(1,128)}), f32[32,1,17472]{2,1,0:T(1,128)S(1)}, u32[]{:S(2)}, u32[]{:S(2)}) %all-to-all-start.1) | async-done | bytes 2236448 | tf_op jit(solution)/shard_map/all_to_all | solution.py:111
  206.0 7.3 %reduce = f32[32,17472]{1,0:T(8,128)} reduce(f32[32,1,17472]{2,1,0:T(1,128)S(1)} %all-to-all-done.1, f32[]{:T(128)} %constant.24), dimensions={1}, to_apply=%all_to_all.62.reduce_sub_computation | reduce | bytes 4472836 | tf_op jit(solution)/shard_map/all_to_all | solution.py:111
  213.3 2.4 reshape.143
  215.8 6.9 %fusion.8 = f32[16,128,128]{1,2,0:T(8,128)S(1)} fusion(f32[16,273,128]{2,1,0:T(8,128)S(1)} %reshape.143, f32[16,256,128]{2,1,0:T(8,128)} %bitcast.119, f32[16,16,128]{2,1,0:T(8,128)} %multiply_bitcast_fusion.1, f32[273]{0:T(512)S(1)} %pad.5.clone), kind=kOutput, calls=%fused_computation.21 | convolution fusion | flops 859901952 | bytes 5514308 | tf_op jit(solution)/shard_map/het,hed->htd/dot_general | solution.py:116
  222.8 1.4 multiply_reduce_fusion.5
  225.3 1.1 copy-done
  226.4 5.3 %fusion.7 = f32[16,273,128]{2,1,0:T(8,128)} fusion(f32[16,128,128]{1,2,0:T(8,128)S(1)} %subtract_multiply_fusion, f32[16,256,128]{2,1,0:T(8,128)S(1)} %bitcast.120, f32[16,16,128]{2,1,0:T(8,128)S(1)} %copy-done.17, f32[273]{0:T(512)S(1)} %pad.5.clone), kind=kOutput, calls=%fused_computation.20 | convolution fusion | flops 859901952 | bytes 5514308 | tf_op jit(solution)/shard_map/het,htd->hed/dot_general | solution.py:120
  231.7 5.2 all_to_all.73
  236.9 58.5 %all_to_all.80 = f32[1,32,17472]{2,0,1:T(1,128)S(1)} all-to-all(f32[1,32,17472]{2,0,1:T(1,128)} %all_to_all.73), channel_id=1, replica_groups=mesh['dp'=8,'ctx'=32] {'ctx'}, dimensions={1} | all-to-all | bytes 4472832 | tf_op jit(solution)/shard_map/all_to_all | solution.py:121
  295.4 1.2 convolution_bitcast_fusion
  296.6 3.8 copy.56
  300.3 5.8 %all-to-all-start.3 = ((f32[32,1,17472]{2,1,0:T(1,128)}), f32[32,1,17472]{2,1,0:T(1,128)}, u32[]{:S(2)}, u32[]{:S(2)}) async-start(f32[32,1,17472]{2,1,0:T(1,128)} %copy.56), calls=%async_computation.3 | async-start | bytes 4489216 | tf_op jit(solution)/shard_map/all_to_all | solution.py:125
  306.1 2.3 copy.57
  308.4 3.9 fusion.61
  313.2 1.0 multiply_reduce_fusion.2
  314.5 1.0 fusion.9
  316.6 1.7 fusion.20
  318.3 40.6 %all-to-all-done.3 = f32[32,1,17472]{2,1,0:T(1,128)} async-done(((f32[32,1,17472]{2,1,0:T(1,128)}), f32[32,1,17472]{2,1,0:T(1,128)}, u32[]{:S(2)}, u32[]{:S(2)}) %all-to-all-start.3) | async-done | bytes 2236448 | tf_op jit(solution)/shard_map/all_to_all | solution.py:125
  358.9 7.7 %all-to-all-start.4 = ((bf16[128,8,512]{0,2,1:T(8,128)(2,1)}), bf16[128,8,512]{0,2,1:T(8,128)(2,1)}, u32[]{:S(2)}, u32[]{:S(2)}) async-start(bf16[128,8,512]{0,2,1:T(8,128)(2,1)} %bitcast.40), calls=%async_computation.4 | async-start | bytes 2097152 | tf_op jit(solution)/shard_map/all_to_all | solution.py:94
  366.8 8.4 %reduce.1 = f32[32,17472]{1,0:T(8,128)} reduce(f32[32,1,17472]{2,1,0:T(1,128)} %all-to-all-done.3, f32[]{:T(128)} %constant.24), dimensions={1}, to_apply=%all_to_all.67.reduce_sub_computation | reduce | bytes 4472836 | tf_op jit(solution)/shard_map/all_to_all | solution.py:125
  375.3 2.2 reshape.146
  377.5 3.1 fusion.27
  380.8 1.1 multiply_reduce_fusion
  382.0 1.0 fusion.19
  384.1 2.3 copy.58
  386.3 32.8 %all-gather.5.cloned.1.call-done = bf16[1024,512]{0,1:T(8,128)(2,1)} async-done(((bf16[128,512]{0,1:T(8,128)(2,1)}), bf16[1024,512]{0,1:T(8,128)(2,1)}) %all-gather.5.cloned.1.call-update) | async-done | bytes 1048592 | tf_op jit(solution)/shard_map/all_gather | solution.py:151
  419.1 3.3 convolution_bitcast_fusion.2
  422.4 2.5 copy.68
  424.9 2.2 fusion.21
  427.1 2.0 copy.59
  429.1 7.0 %fusion.5 = f32[16,128,128]{1,2,0:T(8,128)S(1)} fusion(f32[16,273,128]{2,1,0:T(8,128)S(1)} %reshape.146, f32[16,256,128]{2,1,0:T(8,128)} %bitcast.122, f32[16,16,128]{2,1,0:T(8,128)S(1)} %copy-done.16, f32[273]{0:T(512)} %copy-done.21), kind=kOutput, calls=%fused_computation.18 | convolution fusion | flops 859901952 | bytes 5514308 | tf_op jit(solution)/shard_map/het,hed->htd/dot_general | solution.py:71
  436.1 1.4 fusion.10
  437.5 1.0 copy.60
  438.5 4.7 fusion
  443.2 72.8 %reduce-scatter.4.cloned.1.call-done = f32[16,512]{1,0:T(8,128)} async-done(((f32[512,512]{1,0:T(8,128)}), f32[16,512]{1,0:T(8,128)}) %reduce-scatter.4.cloned.1.call-update) | async-done | bytes 32784
  (64 shorter events, 7.0 us)
Async XLA Ops:
  7.2 58.6 %all-gather.3.cloned.1.call-start = ((), (), s32[]{:S(2)}) async-start(), calls=%async_computation.6 | async-start | bytes 4718592 | tf_op jit(solution)/shard_map/all_gather | solution.py:97
  9.1 60.3 %copy-start.6 = (bf16[16,8,16,128]{3,2,1,0:T(8,128)(2,1)}, bf16[16,8,16,128]{3,2,1,0:T(8,128)(2,1)S(1)}, u32[]{:S(2)}) copy-start(bf16[16,8,16,128]{3,2,1,0:T(8,128)(2,1)S(1)} %copy.72) | copy-start | bytes 1572868
  9.1 216.3 %copy-start.21 = (f32[273]{0:T(512)}, f32[273]{0:T(512)S(1)}, u32[]{:S(2)}) copy-start(f32[273]{0:T(512)S(1)} %pad.5.clone) | copy-start | bytes 3280
  69.1 3.8 copy-start.15
  69.4 1.4 copy-start.1
  147.2 4.6 copy-start.20
  147.2 58.8 %all-to-all-start.1 = ((f32[32,1,17472]{2,1,0:T(1,128)}), f32[32,1,17472]{2,1,0:T(1,128)S(1)}, u32[]{:S(2)}, u32[]{:S(2)}) async-start(f32[32,1,17472]{2,1,0:T(1,128)} %copy.50), calls=%async_computation.1 | async-start | bytes 4489216 | tf_op jit(solution)/shard_map/all_to_all | solution.py:111
  153.1 0.7 copy-start.12
  156.5 66.2 %copy-start.2 = (f32[16,128,128]{2,1,0:T(8,128)}, f32[16,128,128]{2,1,0:T(8,128)S(1)}, u32[]{:S(2)}) copy-start(f32[16,128,128]{2,1,0:T(8,128)S(1)} %fusion.60) | copy-start | bytes 3145732
  215.8 7.0 %copy-start.7 = (bf16[16,8,16,128]{3,2,1,0:T(8,128)(2,1)S(1)}, bf16[16,8,16,128]{3,2,1,0:T(8,128)(2,1)}, u32[]{:S(2)}) copy-start(bf16[16,8,16,128]{3,2,1,0:T(8,128)(2,1)} %copy-done.6) | copy-start | bytes 1572868
  222.7 2.1 copy-start.11
  224.1 1.0 copy-start.5
  224.8 1.6 copy-start
  224.8 1.6 copy-start.17
  300.3 58.6 %all-to-all-start.3 = ((f32[32,1,17472]{2,1,0:T(1,128)}), f32[32,1,17472]{2,1,0:T(1,128)}, u32[]{:S(2)}, u32[]{:S(2)}) async-start(f32[32,1,17472]{2,1,0:T(1,128)} %copy.56), calls=%async_computation.3 | async-start | bytes 4489216 | tf_op jit(solution)/shard_map/all_to_all | solution.py:125
  312.3 0.9 copy-start.13
  313.2 1.2 copy-start.3
  313.2 1.4 copy-start.8
  315.6 1.0 copy-start.9
  358.9 25.1 %all-to-all-start.4 = ((bf16[128,8,512]{0,2,1:T(8,128)(2,1)}), bf16[128,8,512]{0,2,1:T(8,128)(2,1)}, u32[]{:S(2)}, u32[]{:S(2)}) async-start(bf16[128,8,512]{0,2,1:T(8,128)(2,1)} %bitcast.40), calls=%async_computation.4 | async-start | bytes 2097152 | tf_op jit(solution)/shard_map/all_to_all | solution.py:94
  366.6 52.5 %all-gather.5.cloned.1.call-start = ((), (), s32[]{:S(2)}) async-start(), calls=%async_computation.7 | async-start | bytes 1179648 | tf_op jit(solution)/shard_map/all_gather | solution.py:151
  380.8 1.2 copy-start.10
  380.8 1.2 copy-start.14
  383.0 39.3 %copy-start.18 = (bf16[128,16,16]{0,2,1:T(8,128)(2,1)}, bf16[128,16,16]{0,2,1:T(8,128)(2,1)S(1)}, u32[]{:S(2)}) copy-start(bf16[128,16,16]{0,2,1:T(8,128)(2,1)S(1)} %fusion.19) | copy-start | bytes 196612
  383.7 132.2 %reduce-scatter.4.cloned.1.call-start = ((), (), s32[]{:S(2)}) async-start(), calls=%async_computation.8 | async-start | bytes 1081344
  424.9 4.2 copy-start.16
  429.1 7.0 %copy-start.4 = (f32[16,128,128]{2,1,0:T(8,128)S(1)}, f32[16,128,128]{2,1,0:T(8,128)}, u32[]{:S(2)}) copy-start(f32[16,128,128]{2,1,0:T(8,128)} %copy-done.2) | copy-start | bytes 3145732
  436.1 2.4 copy-start.19
Sparse Core Ops, SparseCore 0:
  9.8 55.8 all-gather.2
  383.9 35.1 all-gather.4
  425.0 90.9 reduce-scatter.3
where the time goes:
time: 531 us; the launch traced here: 523 us
  waiting for transfers between devices  250 us (47%)
  blocking collectives  124 us (23%)
  matrix products  50.9 us (10%)
  local copies, waits for them, and re-layouts  38.5 us (7%)
  other arithmetic  26.1 us (5%)
  starting transfers between devices  18.6 us (4%)
  between operations  14.6 us (3%)
    unnamed x4, waiting for transfers between devices  73.5 us
    all_to_all x1, blocking collectives, local(): lax.all_to_all(local_term.reshape(1, -1), 'ctx', split_axis=1, concat_axi...  65.7 us
    all_to_all x1, blocking collectives, local(): lax.all_to_all(carried.reshape(1, -1), 'ctx', split_axis=1, concat_axis=0...  58.5 us
    all_gather x1, waiting for transfers between devices, local(): lax.all_gather(proj_weight, 'dp', axis=0, tiled=True)  56.6 us
    all_to_all x1, waiting for transfers between devices, local(): lax.all_to_all(running, 'ctx', split_axis=0, concat_axis=1, tiled=True)  46.6 us
    all_to_all x1, waiting for transfers between devices, local(): lax.all_to_all(later_running, 'ctx', split_axis=0, concat_axis=1, tiled=T...  40.6 us
    all_gather x1, waiting for transfers between devices, local(): rows_all = lax.all_gather(grad_proj_rows, 'dp', axis=0, tiled=True)  32.8 us
    unnamed x49, local copies, waits for them, and re-layouts  13.7 us
  transfers between devices with their start and end apart: 6, of which 5 were waited for; matrix products, arithmetic and copies ran while one was open for 11% of the time, Pallas kernels for 0%

commit v1 on v0

--- a/solution.py
+++ b/solution.py
@@ -94,7 +94,9 @@
     tokens_cols = lax.all_to_all(token_rows, "dp", split_axis=1, concat_axis=0, tiled=True)
     projected = jnp.dot(
         token_rows,
-        lax.all_gather(proj_weight, "dp", axis=0, tiled=True),
+        jnp.concatenate(
+            lax.all_to_all(jnp.stack([proj_weight] * lax.axis_size("dp")), "dp", 0, 0), axis=0
+        ),
         preferred_element_type=jnp.float32,
     )
     query_part = split_heads(projected[:, :query_cols], F)

time: 531 us -> 583 us (1.098)
  blocking collectives: 124 us -> 166 us
  waiting for transfers between devices: 250 us -> 260 us
    all_to_all x1, waiting for transfers between devices: 0.01 us -> 46.8 us  [local(): lax.all_to_all(jnp.stack([proj_weight] * lax.axis_size('dp')), 'dp', 0, 0)]
    all_to_all x0 -> x1, blocking collectives: none -> 28 us  [local(): lax.all_to_all(token_rows, 'dp', split_axis=1, concat_axis=0, tiled=True)]
    all_gather x1, waiting for transfers between devices: 56.6 us -> 32.6 us  [local(): lax.all_gather(proj_weight, 'dp', axis=0, tiled=True)]
    unnamed x4, waiting for transfers between devices: 73.5 us -> 90.5 us
    all_gather x1, waiting for transfers between devices: 32.8 us -> 17.1 us  [local(): rows_all = lax.all_gather(grad_proj_rows, 'dp', axis=0, tiled=True)]
    all_to_all x1, blocking collectives: 58.5 us -> 72.6 us  [local(): lax.all_to_all(carried.reshape(1, -1), 'ctx', split_axis=1, concat_axis=0...]
    all_to_all x1, waiting for transfers between devices: 46.6 us -> 34.1 us  [local(): lax.all_to_all(running, 'ctx', split_axis=0, concat_axis=1, tiled=True)]
    unnamed x49 -> x53, local copies, waits for them, and re-layouts: 13.7 us -> 12.7 us
  transfers between devices with their start and end apart: 6 -> 6, of which waited for: 5 -> 6; matrix products, arithmetic and copies ran while one was open for 11% -> 8% of each run, Pallas kernels for 0% -> 0%
where the time goes in v1:
time: 583 us; the launch traced here: 575 us
  waiting for transfers between devices  260 us (45%)
  blocking collectives  166 us (28%)
  matrix products  50.6 us (9%)
  local copies, waits for them, and re-layouts  40.7 us (7%)
  other arithmetic  26.4 us (5%)
  starting transfers between devices  16.9 us (3%)
  between operations  14.5 us (2%)
    unnamed x4, waiting for transfers between devices  90.5 us
    all_to_all x1, blocking collectives, local(): lax.all_to_all(carried.reshape(1, -1), 'ctx', split_axis=1, concat_axis=0...  72.6 us
    all_to_all x1, blocking collectives, local(): lax.all_to_all(local_term.reshape(1, -1), 'ctx', split_axis=1, concat_axi...  65.4 us
    all_to_all x1, waiting for transfers between devices, local(): lax.all_to_all(jnp.stack([proj_weight] * lax.axis_size('dp')), 'dp', 0, 0)  46.8 us
    all_to_all x1, waiting for transfers between devices, local(): lax.all_to_all(later_running, 'ctx', split_axis=0, concat_axis=1, tiled=T...  38.9 us
    all_to_all x1, waiting for transfers between devices, local(): lax.all_to_all(running, 'ctx', split_axis=0, concat_axis=1, tiled=True)  34.1 us
    all_gather x1, waiting for transfers between devices, local(): lax.all_gather(proj_weight, 'dp', axis=0, tiled=True)  32.6 us
    all_to_all x1, blocking collectives, local(): lax.all_to_all(token_rows, 'dp', split_axis=1, concat_axis=0, tiled=True)  28 us
  transfers between devices with their start and end apart: 6, of which 6 were waited for; matrix products, arithmetic and copies ran while one was open for 8% of the time, Pallas kernels for 0%

profile of v1, /device:TPU:2, one launch (start us, length us, event | category | flops | bytes accessed | tf_op | source)
XLA Modules:
  0.0 575.1 jit_solution(857788739389551473)
XLA Ops:
  7.2 3.4 stack.2
  10.6 6.8 %all-to-all-start = ((bf16[8,512,512]{2,1,0:T(8,128)(2,1)}), bf16[8,512,512]{2,1,0:T(8,128)(2,1)}, u32[]{:S(2)}, u32[]{:S(2)}) async-start(bf16[8,512,512]{2,1,0:T(8,128)(2,1)} %stack.2), calls=%async_computation | async-start | bytes 8388608 | tf_op jit(solution)/shard_map/all_to_all | solution.py:98
  17.5 46.8 %all-to-all-done = bf16[8,512,512]{2,1,0:T(8,128)(2,1)} async-done(((bf16[8,512,512]{2,1,0:T(8,128)(2,1)}), bf16[8,512,512]{2,1,0:T(8,128)(2,1)}, u32[]{:S(2)}, u32[]{:S(2)}) %all-to-all-start) | async-done | bytes 4194336 | tf_op jit(solution)/shard_map/all_to_all | solution.py:98
  64.3 2.9 fusion.22
  67.7 1.3 copy-done.1
  69.0 2.1 fusion.6
  71.1 3.7 all_to_all.76
  74.8 65.4 %all_to_all.84 = f32[1,32,17472]{2,0,1:T(1,128)S(1)} all-to-all(f32[1,32,17472]{2,0,1:T(1,128)} %all_to_all.76), channel_id=1, replica_groups=mesh['dp'=8,'ctx'=32] {'ctx'}, dimensions={1} | all-to-all | bytes 4472832 | tf_op jit(solution)/shard_map/all_to_all | solution.py:109
  140.2 1.2 convolution_bitcast_fusion.1
  141.4 3.8 copy.50
  145.1 5.1 all-to-all-start.2
  150.2 1.2 copy.51
  152.2 2.7 fusion.60
  154.9 2.9 multiply_multiply_fusion.1
  157.9 34.1 %all-to-all-done.2 = f32[32,1,17472]{2,1,0:T(1,128)S(1)} async-done(((f32[32,1,17472]{2,1,0:T(1,128)}), f32[32,1,17472]{2,1,0:T(1,128)S(1)}, u32[]{:S(2)}, u32[]{:S(2)}) %all-to-all-start.2) | async-done | bytes 2236448 | tf_op jit(solution)/shard_map/all_to_all | solution.py:113
  191.9 7.4 %reduce = f32[32,17472]{1,0:T(8,128)} reduce(f32[32,1,17472]{2,1,0:T(1,128)S(1)} %all-to-all-done.2, f32[]{:T(128)} %constant.24), dimensions={1}, to_apply=%all_to_all.66.reduce_sub_computation | reduce | bytes 4472836 | tf_op jit(solution)/shard_map/all_to_all | solution.py:113
  199.3 2.7 reshape.149
  202.0 6.9 %fusion.8 = f32[16,128,128]{1,2,0:T(8,128)S(1)} fusion(f32[16,273,128]{2,1,0:T(8,128)S(1)} %reshape.149, f32[16,256,128]{2,1,0:T(8,128)} %bitcast.120, f32[16,16,128]{2,1,0:T(8,128)} %multiply_bitcast_fusion.1, f32[273]{0:T(512)S(1)} %pad.5.clone), kind=kOutput, calls=%fused_computation.21 | convolution fusion | flops 859901952 | bytes 5514308 | tf_op jit(solution)/shard_map/het,hed->htd/dot_general | solution.py:118
  209.0 1.4 multiply_reduce_fusion.5
  211.5 1.0 copy-done
  212.6 5.3 fusion.7
  217.9 4.9 all_to_all.77
  222.8 72.6 %all_to_all.85 = f32[1,32,17472]{2,0,1:T(1,128)S(1)} all-to-all(f32[1,32,17472]{2,0,1:T(1,128)} %all_to_all.77), channel_id=1, replica_groups=mesh['dp'=8,'ctx'=32] {'ctx'}, dimensions={1} | all-to-all | bytes 4472832 | tf_op jit(solution)/shard_map/all_to_all | solution.py:123
  295.4 1.2 convolution_bitcast_fusion
  296.6 3.7 copy.56
  300.3 4.9 all-to-all-start.4
  305.2 3.9 fusion.61
  311.4 1.0 fusion.9
  313.3 1.7 fusion.20
  315.1 38.9 %all-to-all-done.4 = f32[32,1,17472]{2,1,0:T(1,128)} async-done(((f32[32,1,17472]{2,1,0:T(1,128)}), f32[32,1,17472]{2,1,0:T(1,128)}, u32[]{:S(2)}, u32[]{:S(2)}) %all-to-all-start.4) | async-done | bytes 2236448 | tf_op jit(solution)/shard_map/all_to_all | solution.py:127
  354.0 8.6 %reduce.1 = f32[32,17472]{1,0:T(8,128)} reduce(f32[32,1,17472]{2,1,0:T(1,128)} %all-to-all-done.4, f32[]{:T(128)} %constant.24), dimensions={1}, to_apply=%all_to_all.71.reduce_sub_computation | reduce | bytes 4472836 | tf_op jit(solution)/shard_map/all_to_all | solution.py:127
  362.6 2.2 reshape.152
  364.8 3.1 fusion.27
  368.2 1.1 multiply_reduce_fusion
  371.9 2.3 copy.57
  374.2 28.0 %all_to_all.86 = bf16[128,8,512]{0,2,1:T(8,128)(2,1)} all-to-all(bf16[128,8,512]{0,2,1:T(8,128)(2,1)} %bitcast.143), channel_id=1, replica_groups=mesh['dp'=8,'ctx'=32] {'dp'}, dimensions={1} | all-to-all | bytes 2097152 | tf_op jit(solution)/shard_map/all_to_all | solution.py:94
  402.2 2.3 copy.58
  404.5 17.1 %all-gather.5.cloned.1.call-done = bf16[1024,512]{0,1:T(8,128)(2,1)} async-done(((bf16[128,512]{0,1:T(8,128)(2,1)}), bf16[1024,512]{0,1:T(8,128)(2,1)}) %all-gather.5.cloned.1.call-update) | async-done | bytes 1048592 | tf_op jit(solution)/shard_map/all_gather | solution.py:153
  421.6 3.3 convolution_bitcast_fusion.2
  424.8 2.6 copy.68
  427.5 2.2 fusion.21
  429.7 2.0 copy.59
  431.7 7.0 %fusion.5 = f32[16,128,128]{1,2,0:T(8,128)S(1)} fusion(f32[16,273,128]{2,1,0:T(8,128)S(1)} %reshape.152, f32[16,256,128]{2,1,0:T(8,128)} %bitcast.123, f32[16,16,128]{2,1,0:T(8,128)S(1)} %copy-done.17, f32[273]{0:T(512)} %copy-done.23), kind=kOutput, calls=%fused_computation.18 | convolution fusion | flops 859901952 | bytes 5514308 | tf_op jit(solution)/shard_map/het,hed->htd/dot_general | solution.py:71
  438.8 1.4 fusion.10
  440.1 1.0 copy.60
  441.1 32.6 %all-gather.3.cloned.1.call-done = bf16[4096,512]{1,0:T(8,128)(2,1)} async-done(((bf16[512,512]{1,0:T(8,128)(2,1)}), bf16[4096,512]{1,0:T(8,128)(2,1)}) %all-gather.3.cloned.1.call-update) | async-done | bytes 4194320 | tf_op jit(solution)/shard_map/all_gather | solution.py:149
  473.8 4.7 fusion
  478.4 89.8 %reduce-scatter.4.cloned.1.call-done = f32[16,512]{1,0:T(8,128)} async-done(((f32[512,512]{1,0:T(8,128)}), f32[16,512]{1,0:T(8,128)}) %reduce-scatter.4.cloned.1.call-update) | async-done | bytes 32784
  (70 shorter events, 8.7 us)
Async XLA Ops:
  10.6 6.8 %copy-start.22 = (bf16[1,128,2048]{2,1,0:T(8,128)(2,1)S(1)}, bf16[1,128,2048]{2,1,0:T(8,128)(2,1)}, u32[]{:S(2)}) copy-start(bf16[1,128,2048]{2,1,0:T(8,128)(2,1)} %param.6) | copy-start | bytes 1572868
  10.6 53.8 %copy-start.15 = (bf16[1,128,4096]{2,1,0:T(8,128)(2,1)S(1)}, bf16[1,128,4096]{2,1,0:T(8,128)(2,1)}, u32[]{:S(2)}) copy-start(bf16[1,128,4096]{2,1,0:T(8,128)(2,1)} %param.4) | copy-start | bytes 3145732
  10.6 53.8 %all-to-all-start = ((bf16[8,512,512]{2,1,0:T(8,128)(2,1)}), bf16[8,512,512]{2,1,0:T(8,128)(2,1)}, u32[]{:S(2)}, u32[]{:S(2)}) async-start(bf16[8,512,512]{2,1,0:T(8,128)(2,1)} %stack.2), calls=%async_computation | async-start | bytes 8388608 | tf_op jit(solution)/shard_map/all_to_all | solution.py:98
  17.5 50.2 %copy-start.6 = (bf16[16,8,16,128]{3,2,1,0:T(8,128)(2,1)}, bf16[16,8,16,128]{3,2,1,0:T(8,128)(2,1)S(1)}, u32[]{:S(2)}) copy-start(bf16[16,8,16,128]{3,2,1,0:T(8,128)(2,1)S(1)} %copy.72) | copy-start | bytes 1572868
  17.5 194.0 %copy-start.23 = (f32[273]{0:T(512)}, f32[273]{0:T(512)S(1)}, u32[]{:S(2)}) copy-start(f32[273]{0:T(512)S(1)} %pad.5.clone) | copy-start | bytes 3280
  67.6 1.3 copy-start.1
  67.7 3.4 copy-start.16
  145.1 5.1 copy-start.21
  145.1 46.8 %all-to-all-start.2 = ((f32[32,1,17472]{2,1,0:T(1,128)}), f32[32,1,17472]{2,1,0:T(1,128)S(1)}, u32[]{:S(2)}, u32[]{:S(2)}) async-start(f32[32,1,17472]{2,1,0:T(1,128)} %copy.50), calls=%async_computation.2 | async-start | bytes 4489216 | tf_op jit(solution)/shard_map/all_to_all | solution.py:113
  151.5 0.7 copy-start.12
  154.9 54.0 %copy-start.2 = (f32[16,128,128]{2,1,0:T(8,128)}, f32[16,128,128]{2,1,0:T(8,128)S(1)}, u32[]{:S(2)}) copy-start(f32[16,128,128]{2,1,0:T(8,128)S(1)} %fusion.60) | copy-start | bytes 3145732
  202.0 7.0 %copy-start.7 = (bf16[16,8,16,128]{3,2,1,0:T(8,128)(2,1)S(1)}, bf16[16,8,16,128]{3,2,1,0:T(8,128)(2,1)}, u32[]{:S(2)}) copy-start(bf16[16,8,16,128]{3,2,1,0:T(8,128)(2,1)} %copy-done.6) | copy-start | bytes 1572868
  208.9 2.1 copy-start.9
  210.3 1.0 copy-start.5
  211.0 1.6 copy-start
  211.0 1.6 copy-start.18
  300.3 53.7 %all-to-all-start.4 = ((f32[32,1,17472]{2,1,0:T(1,128)}), f32[32,1,17472]{2,1,0:T(1,128)}, u32[]{:S(2)}, u32[]{:S(2)}) async-start(f32[32,1,17472]{2,1,0:T(1,128)} %copy.56), calls=%async_computation.4 | async-start | bytes 4489216 | tf_op jit(solution)/shard_map/all_to_all | solution.py:127
  305.2 116.4 %all-gather.5.cloned.1.call-start = ((), (), s32[]{:S(2)}) async-start(), calls=%async_computation.8 | async-start | bytes 1179648 | tf_op jit(solution)/shard_map/all_gather | solution.py:153
  309.1 0.9 copy-start.13
  310.0 1.2 copy-start.3
  310.0 1.4 copy-start.8
  312.4 1.0 copy-start.10
  368.2 1.2 copy-start.11
  368.2 1.2 copy-start.14
  370.4 31.8 %copy-start.19 = (bf16[128,16,16]{0,2,1:T(8,128)(2,1)}, bf16[128,16,16]{0,2,1:T(8,128)(2,1)S(1)}, u32[]{:S(2)}) copy-start(bf16[128,16,16]{0,2,1:T(8,128)(2,1)S(1)} %fusion.19) | copy-start | bytes 196612
  371.1 102.6 %all-gather.3.cloned.1.call-start = ((), (), s32[]{:S(2)}) async-start(), calls=%async_computation.7 | async-start | bytes 4718592 | tf_op jit(solution)/shard_map/all_gather | solution.py:149
  371.9 196.3 %reduce-scatter.4.cloned.1.call-start = ((), (), s32[]{:S(2)}) async-start(), calls=%async_computation.9 | async-start | bytes 1081344
  427.5 4.2 copy-start.17
  431.7 7.0 %copy-start.4 = (f32[16,128,128]{2,1,0:T(8,128)S(1)}, f32[16,128,128]{2,1,0:T(8,128)}, u32[]{:S(2)}) copy-start(f32[16,128,128]{2,1,0:T(8,128)} %copy-done.2) | copy-start | bytes 3145732
  438.8 35.0 %copy-start.20 = (bf16[128,16,16]{0,2,1:T(8,128)(2,1)S(1)}, bf16[128,16,16]{0,2,1:T(8,128)(2,1)}, u32[]{:S(2)}) copy-start(bf16[128,16,16]{0,2,1:T(8,128)(2,1)} %copy-done.19) | copy-start | bytes 196612
Sparse Core Ops, SparseCore 0:
  371.2 50.2 all-gather.4
  423.4 50.3 all-gather.2
  478.1 90.0 reduce-scatter.3
